TPU v7x, 32 devices: a whole 2x2x4 slice. The times are simulated.
32 devices in a mesh: ia: 4 (over z), ja: 4 (over x, core), ka: 2 (over y).
Axes of the slice: x: 2, y: 2, z: 4, core: 2. Of those that a mesh axis runs over, the one named last changes fastest.
Arguments:
- tensor: bfloat16 [64, 256, 512], P('ka', 'ia', 'ja'), may hold values from -768 to 768
- observed: int32 [64, 256, 512], P('ka', 'ia', 'ja'), may hold values from 0 to 1, as said below
- factor_a: bfloat16 [256, 128], P('ia', ('ja', 'ka')), may hold values from -6 to 6
- factor_b: bfloat16 [512, 128], P('ja', ('ia', 'ka')), may hold values from -6 to 6
- factor_c: bfloat16 [64, 128], P('ka', ('ia', 'ja')), may hold values from -6 to 6
Outputs:
- step_a: float32 [256, 128], P('ia', ('ja', 'ka'))
- step_b: float32 [512, 128], P('ja', ('ia', 'ka'))
- step_c: float32 [64, 128], P('ka', ('ia', 'ja'))
Inputs may be any that keep to these rules, and one draw needn't show every extreme that they name: `observed`: a 0/1 weight per cell.
All inputs are finite; a program needn't handle non-finite values.
Results may differ from a plain program's by a relative error of at most 0.0095.
Values may be sent and summed in bfloat16 or wider, within the bound.
A program may use at most 64 MiB of HBM per device.

v0:
```python
import jax
import jax.numpy as jnp
from jax import lax
from jax.sharding import PartitionSpec as P

ITERS = 2
DAMP = 1.0


def against(left_side, right_side):
    return lax.dot_general(
        left_side, right_side, (((1,), (1,)), ((), ())), preferred_element_type=jnp.float32
    )


def local(tensor, observed, factor_a, factor_b, factor_c):
    depth_rows, height_rows, width_cols = tensor.shape
    divisor = width_cols * lax.axis_size("ja") * (depth_rows * lax.axis_size("ka")) / 32.0
    full_a = lax.all_gather(factor_a, ("ja", "ka"), axis=1, tiled=True)
    full_b = lax.all_gather(factor_b, ("ia", "ka"), axis=1, tiled=True)
    full_c = lax.all_gather(factor_c, ("ia", "ja"), axis=1, tiled=True)
    columns = full_a.shape[1]
    wide_a = full_a.astype(jnp.float32)
    wide_c = full_c.astype(jnp.float32)
    weight = (observed.astype(jnp.float32) * (1.0 / divisor)).astype(jnp.bfloat16)
    weight = weight.reshape(depth_rows * height_rows, width_cols)
    paired = (
        (wide_c[:, None, :] * wide_a[None, :, :])
        .astype(jnp.bfloat16)
        .reshape(depth_rows * height_rows, columns)
    )

    def partials(weighted):
        part_b = lax.dot_general(
            weighted, paired, (((0,), (0,)), ((), ())), preferred_element_type=jnp.float32
        )
        mixture = jnp.dot(weighted, full_b, preferred_element_type=jnp.float32).reshape(
            depth_rows, height_rows, columns
        )
        part_a = jnp.einsum("kir,kr->ir", mixture, wide_c)
        part_c = jnp.einsum("kir,ir->kr", mixture, wide_a)
        return (part_a, part_b, part_c)

    def settle(parts):
        total_a = lax.psum(parts[0], ("ja", "ka"))
        total_b = lax.psum(parts[1], ("ia", "ka"))
        total_c = lax.psum(parts[2], ("ia", "ja"))
        return (total_a, total_b, total_c)

    scales = (
        1.0 / lax.axis_size(("ja", "ka")),
        1.0 / lax.axis_size(("ia", "ka")),
        1.0 / lax.axis_size(("ia", "ja")),
    )

    def inner_sum(first, second):
        local_sum = sum(
            (
                jnp.sum(left_side * right_side) * factor
                for left_side, right_side, factor in zip(first, second, scales)
            )
        )
        return lax.psum(local_sum, ("ia", "ja", "ka"))

    def expand(direction):
        hat_a = direction[0].astype(jnp.bfloat16)
        hat_b = direction[1].astype(jnp.bfloat16)
        hat_c = direction[2].astype(jnp.bfloat16)
        return (hat_a, hat_b, hat_c)

    def hessian_times(direction):
        hat_a, hat_b, hat_c = expand(direction)
        sideways = (
            hat_c.astype(jnp.float32)[:, None, :] * wide_a[None, :, :]
            + wide_c[:, None, :] * hat_a.astype(jnp.float32)[None, :, :]
        )
        sideways = sideways.astype(jnp.bfloat16).reshape(depth_rows * height_rows, columns)
        tangent = against(paired, hat_b) + against(sideways, full_b)
        weighted = (weight.astype(jnp.float32) * tangent).astype(jnp.bfloat16)
        parts = settle(partials(weighted))
        return tuple((part + DAMP * vector for part, vector in zip(parts, direction)))

    fitted = against(paired, full_b)
    values = tensor.reshape(depth_rows * height_rows, width_cols).astype(jnp.float32)
    errors = (weight.astype(jnp.float32) * (values - fitted)).astype(jnp.bfloat16)
    gradient = settle(partials(errors))
    solution = tuple((jnp.zeros_like(vector) for vector in gradient))
    residual = gradient
    direction = gradient
    norm_now = inner_sum(residual, residual)
    for iteration in range(ITERS):
        product = hessian_times(direction)
        step_size = norm_now / inner_sum(direction, product)
        solution = tuple(
            (vector + step_size * update for vector, update in zip(solution, direction))
        )
        if iteration + 1 < ITERS:
            residual = tuple(
                (vector - step_size * update for vector, update in zip(residual, product))
            )
            norm_next = inner_sum(residual, residual)
            direction = tuple(
                (
                    vector + norm_next / norm_now * update
                    for vector, update in zip(residual, direction)
                )
            )
            norm_now = norm_next
    position_a = lax.axis_index(("ja", "ka")) * factor_a.shape[1]
    position_b = lax.axis_index(("ia", "ka")) * factor_b.shape[1]
    position_c = lax.axis_index(("ia", "ja")) * factor_c.shape[1]
    step_a = lax.dynamic_slice_in_dim(solution[0], position_a, factor_a.shape[1], 1)
    step_b = lax.dynamic_slice_in_dim(solution[1], position_b, factor_b.shape[1], 1)
    step_c = lax.dynamic_slice_in_dim(solution[2], position_c, factor_c.shape[1], 1)
    return (step_a, step_b, step_c)


def solution(mesh):
    placed = (
        P("ka", "ia", "ja"),
        P("ka", "ia", "ja"),
        P("ia", ("ja", "ka")),
        P("ja", ("ia", "ka")),
        P("ka", ("ia", "ja")),
    )
    return jax.shard_map(
        local,
        mesh=mesh,
        in_specs=placed,
        out_specs=(P("ia", ("ja", "ka")), P("ja", ("ia", "ka")), P("ka", ("ia", "ja"))),
        check_vma=False,
    )
```

profile of v0, /device:TPU:0, one launch (start us, length us, event | category | flops | bytes accessed | tf_op | source)
XLA Modules:
  0.0 519.4 jit_solution(12304898515846047202)
XLA Ops:
  7.2 14.5 %all_gather.10 = bf16[64,128]{0,1:T(8,128)(2,1)S(1)} all-gather(bf16[64,16]{0,1:T(8,128)(2,1)} %param.7), channel_id=1, replica_groups=mesh['ia'=4,'ja'=4,'ka'=2] {'ja','ka'}, dimensions={1}, use_global_device_ids=true | all-gather | bytes 18432 | tf_op jit(solution)/shard_map/all_gather | solution.py:19
  22.4 21.9 %all_gather.9 = bf16[32,128]{0,1:T(8,128)(2,1)S(1)} all-gather(bf16[32,8]{0,1:T(8,128)(2,1)S(1)} %copy-done.3), channel_id=1, replica_groups=mesh['ia'=4,'ja'=4,'ka'=2] {'ia','ja'}, dimensions={1}, use_global_device_ids=true | all-gather | bytes 8704 | tf_op jit(solution)/shard_map/all_gather | solution.py:21
  44.4 0.7 copy-done.2
  45.1 30.6 %all_gather.11 = bf16[128,128]{0,1:T(8,128)(2,1)S(1)} all-gather(bf16[128,16]{0,1:T(8,128)(2,1)S(1)} %copy-done.2), channel_id=1, replica_groups=mesh['ia'=4,'ja'=4,'ka'=2] {'ia','ka'}, dimensions={1}, use_global_device_ids=true | all-gather | bytes 36864 | tf_op jit(solution)/shard_map/all_gather | solution.py:20
  75.7 1.4 multiply_convert_fusion.1
  77.2 0.9 copy-done.1
  78.4 1.0 fusion.16
  80.1 22.7 %psum.91 = f32[64,128]{1,0:T(8,128)S(1)} all-reduce(f32[64,128]{1,0:T(8,128)S(1)} %bitcast.75), channel_id=1, replica_groups=mesh['ia'=4,'ja'=4,'ka'=2] {'ja','ka'}, use_global_device_ids=true, to_apply=%region_0.0 | all-reduce | flops 8192 | bytes 65536 | tf_op jit(solution)/shard_map/psum | solution.py:45
  102.8 58.1 %psum.93 = f32[32,128]{1,0:T(8,128)S(1)} all-reduce(f32[32,128]{1,0:T(8,128)S(1)} %bitcast.78), channel_id=1, replica_groups=mesh['ia'=4,'ja'=4,'ka'=2] {'ia','ja'}, use_global_device_ids=true, to_apply=%region_4.0 | all-reduce | flops 4096 | bytes 32768 | tf_op jit(solution)/shard_map/psum | solution.py:47
  161.0 1.1 fusion.12
  162.5 1.0 fusion.17
  164.0 23.9 %psum.95 = f32[64,128]{1,0:T(8,128)S(1)} all-reduce(f32[64,128]{1,0:T(8,128)S(1)} %bitcast.76), channel_id=1, replica_groups=mesh['ia'=4,'ja'=4,'ka'=2] {'ja','ka'}, use_global_device_ids=true, to_apply=%region_7.0 | all-reduce | flops 8192 | bytes 65536 | tf_op jit(solution)/shard_map/psum | solution.py:45
  188.4 57.7 %psum.97 = f32[32,128]{1,0:T(8,128)S(1)} all-reduce(f32[32,128]{1,0:T(8,128)S(1)} %bitcast.77), channel_id=1, replica_groups=mesh['ia'=4,'ja'=4,'ka'=2] {'ia','ja'}, use_global_device_ids=true, to_apply=%region_11.0 | all-reduce | flops 4096 | bytes 32768 | tf_op jit(solution)/shard_map/psum | solution.py:47
  246.2 0.7 multiply_reduce_fusion.13
  248.1 1.5 multiply_reduce_fusion.7
  252.3 36.9 %all-reduce = (f32[]{:T(128)}, f32[]{:T(128)}) all-reduce(f32[]{:T(128)S(6)} %add.125, f32[]{:T(128)S(6)} %add.132), channel_id=1, replica_groups=mesh['ia'=4,'ja'=4,'ka'=2] {'ia','ja','ka'}, use_global_device_ids=true, to_apply=%region_6.0 | all-reduce | flops 2 | bytes 16 | tf_op jit(solution)/shard_map/psum | solution.py:63
  294.3 41.9 %psum.99 = f32[]{:T(128)} all-reduce(f32[]{:T(128)S(6)} %add.134), channel_id=1, replica_groups=mesh['ia'=4,'ja'=4,'ka'=2] {'ia','ja','ka'}, use_global_device_ids=true, to_apply=%region_17.0 | all-reduce | flops 1 | bytes 8 | tf_op jit(solution)/shard_map/psum | solution.py:63
  338.7 1.0 fusion.18
  339.6 59.3 %psum.102 = f32[32,128]{1,0:T(8,128)S(1)} all-reduce(f32[32,128]{1,0:T(8,128)S(1)} %bitcast.79), channel_id=1, replica_groups=mesh['ia'=4,'ja'=4,'ka'=2] {'ia','ja'}, use_global_device_ids=true, to_apply=%region_22.0 | all-reduce | flops 4096 | bytes 32768 | tf_op jit(solution)/shard_map/psum | solution.py:47
  400.3 23.2 %psum.100 = f32[64,128]{1,0:T(8,128)S(1)} all-reduce(f32[64,128]{1,0:T(8,128)S(1)} %bitcast.74), channel_id=1, replica_groups=mesh['ia'=4,'ja'=4,'ka'=2] {'ja','ka'}, use_global_device_ids=true, to_apply=%region_18.0 | all-reduce | flops 8192 | bytes 65536 | tf_op jit(solution)/shard_map/psum | solution.py:45
  424.1 42.1 %all-reduce.9.cloned.1.call-done = f32[128,128]{1,0:T(8,128)} async-done(((f32[128,128]{1,0:T(8,128)}), f32[128,128]{1,0:T(8,128)}) %all-reduce.9.cloned.1.call-update) | async-done | bytes 65552 | tf_op jit(solution)/shard_map/psum | solution.py:46
  466.2 1.5 fusion.6
  469.0 40.3 %psum.103 = f32[]{:T(128)} all-reduce(f32[]{:T(128)S(6)} %add.144), channel_id=1, replica_groups=mesh['ia'=4,'ja'=4,'ka'=2] {'ia','ja','ka'}, use_global_device_ids=true, to_apply=%region_24.0 | all-reduce | flops 1 | bytes 8 | tf_op jit(solution)/shard_map/psum | solution.py:63
  512.2 0.7 copy.22
  (51 shorter events, 9.5 us)
Async XLA Ops:
  7.2 153.9 %all-reduce.5.cloned.1.call-start = ((), (), s32[]{:S(2)}) async-start(), calls=%async_computation | async-start | bytes 131072 | tf_op jit(solution)/shard_map/psum | solution.py:46
  21.8 0.7 copy-start.3
  44.4 0.7 copy-start.2
  77.0 1.0 copy-start.1
  79.4 168.7 %all-reduce.7.cloned.1.call-start = ((), (), s32[]{:S(2)}) async-start(), calls=%async_computation.1 | async-start | bytes 131072 | tf_op jit(solution)/shard_map/psum | solution.py:46
  163.8 302.5 %all-reduce.9.cloned.1.call-start = ((), (), s32[]{:S(2)}) async-start(), calls=%async_computation.2 | async-start | bytes 131072 | tf_op jit(solution)/shard_map/psum | solution.py:46
  188.4 59.7 %copy-start = (f32[128,128]{1,0:T(8,128)S(1)}, f32[128,128]{1,0:T(8,128)}, u32[]{:S(2)}) copy-start(f32[128,128]{1,0:T(8,128)} %all-reduce.5.cloned.1.call-done) | copy-start | bytes 196612
Sparse Core Ops, SparseCore 0:
  79.5 66.1 all-reduce.4
  163.9 66.5 all-reduce.6
  400.3 65.8 all-reduce.8
where the time goes:
time: 520 us; the launch traced here: 519 us
  blocking collectives  431 us (83%)
  waiting for transfers between devices  42.2 us (8%)
  between operations  25.8 us (5%)
  other arithmetic  9.88 us (2%)
  matrix products  6.15 us (1%)
    psum x3, blocking collectives, settle(): total_c = lax.psum(parts[2], ('ia', 'ja'))  175 us
    psum x3, blocking collectives, inner_sum(): return lax.psum(local_sum, ('ia', 'ja', 'ka'))  119 us
    psum x3, blocking collectives, settle(): total_a = lax.psum(parts[0], ('ja', 'ka'))  69.7 us
    psum x3, waiting for transfers between devices, settle(): total_b = lax.psum(parts[1], ('ia', 'ka'))  42.1 us
    all_gather x1, blocking collectives, local(): full_b = lax.all_gather(factor_b, ('ia', 'ka'), axis=1, tiled=True)  30.6 us
    all_gather x1, blocking collectives, local(): full_c = lax.all_gather(factor_c, ('ia', 'ja'), axis=1, tiled=True)  21.9 us
    all_gather x1, blocking collectives, local(): full_a = lax.all_gather(factor_a, ('ja', 'ka'), axis=1, tiled=True)  14.5 us
  transfers between devices with their start and end apart: 3, of which 1 were waited for; matrix products, arithmetic and copies ran while one was open for 1% of the time, Pallas kernels for 0%

commit v1 on v0

--- a/solution.py
+++ b/solution.py
@@ -43,7 +43,7 @@
 
     def settle(parts):
         total_a = lax.psum(parts[0], ("ja", "ka"))
-        total_b = lax.psum(parts[1], ("ia", "ka"))
+        total_b = lax.psum(lax.psum(parts[1], "ka"), "ia")
         total_c = lax.psum(parts[2], ("ia", "ja"))
         return (total_a, total_b, total_c)
 

time: 520 us -> 573 us (1.10)
  waiting for transfers between devices: 42.2 us -> 91.5 us
    psum x3 -> x6, waiting for transfers between devices: 42.1 us -> 91.4 us  [settle(): total_b = lax.psum(lax.psum(parts[1], 'ka'), 'ia')]
  transfers between devices with their start and end apart: 3 -> 6, of which waited for: 1 -> 3; matrix products, arithmetic and copies ran while one was open for 1% -> 1% of each run, Pallas kernels for 0% -> 0%
where the time goes in v1:
time: 573 us; the launch traced here: 572 us
  blocking collectives  434 us (76%)
  waiting for transfers between devices  91.5 us (16%)
  between operations  26.2 us (5%)
  other arithmetic  9.88 us (2%)
  matrix products  6.15 us (1%)
    psum x3, blocking collectives, settle(): total_c = lax.psum(parts[2], ('ia', 'ja'))  178 us
    psum x3, blocking collectives, inner_sum(): return lax.psum(local_sum, ('ia', 'ja', 'ka'))  119 us
    psum x6, waiting for transfers between devices, settle(): total_b = lax.psum(lax.psum(parts[1], 'ka'), 'ia')  91.4 us
    psum x3, blocking collectives, settle(): total_a = lax.psum(parts[0], ('ja', 'ka'))  69.2 us
    all_gather x1, blocking collectives, local(): full_b = lax.all_gather(factor_b, ('ia', 'ka'), axis=1, tiled=True)  30.6 us
    all_gather x1, blocking collectives, local(): full_c = lax.all_gather(factor_c, ('ia', 'ja'), axis=1, tiled=True)  21.9 us
    all_gather x1, blocking collectives, local(): full_a = lax.all_gather(factor_a, ('ja', 'ka'), axis=1, tiled=True)  14.5 us
  transfers between devices with their start and end apart: 6, of which 3 were waited for; matrix products, arithmetic and copies ran while one was open for 1% of the time, Pallas kernels for 0%

profile of v1, /device:TPU:0, one launch (start us, length us, event | category | flops | bytes accessed | tf_op | source)
XLA Modules:
  0.0 572.4 jit_solution(304773239386209187)
XLA Ops:
  7.2 14.5 %all_gather.10 = bf16[64,128]{0,1:T(8,128)(2,1)S(1)} all-gather(bf16[64,16]{0,1:T(8,128)(2,1)} %param.7), channel_id=1, replica_groups=mesh['ia'=4,'ja'=4,'ka'=2] {'ja','ka'}, dimensions={1}, use_global_device_ids=true | all-gather | bytes 18432 | tf_op jit(solution)/shard_map/all_gather | solution.py:19
  22.4 21.9 %all_gather.9 = bf16[32,128]{0,1:T(8,128)(2,1)S(1)} all-gather(bf16[32,8]{0,1:T(8,128)(2,1)S(1)} %copy-done.3), channel_id=1, replica_groups=mesh['ia'=4,'ja'=4,'ka'=2] {'ia','ja'}, dimensions={1}, use_global_device_ids=true | all-gather | bytes 8704 | tf_op jit(solution)/shard_map/all_gather | solution.py:21
  44.4 0.7 copy-done.2
  45.1 30.6 %all_gather.11 = bf16[128,128]{0,1:T(8,128)(2,1)S(1)} all-gather(bf16[128,16]{0,1:T(8,128)(2,1)S(1)} %copy-done.2), channel_id=1, replica_groups=mesh['ia'=4,'ja'=4,'ka'=2] {'ia','ka'}, dimensions={1}, use_global_device_ids=true | all-gather | bytes 36864 | tf_op jit(solution)/shard_map/all_gather | solution.py:20
  75.7 1.4 multiply_convert_fusion.1
  77.2 0.9 copy-done.1
  78.4 1.0 fusion.16
  80.1 22.5 %psum.112 = f32[64,128]{1,0:T(8,128)S(1)} all-reduce(f32[64,128]{1,0:T(8,128)S(1)} %bitcast.75), channel_id=1, replica_groups=mesh['ia'=4,'ja'=4,'ka'=2] {'ja','ka'}, use_global_device_ids=true, to_apply=%region_0.0 | all-reduce | flops 8192 | bytes 65536 | tf_op jit(solution)/shard_map/psum | solution.py:45
  102.6 58.1 %psum.115 = f32[32,128]{1,0:T(8,128)S(1)} all-reduce(f32[32,128]{1,0:T(8,128)S(1)} %bitcast.78), channel_id=1, replica_groups=mesh['ia'=4,'ja'=4,'ka'=2] {'ia','ja'}, use_global_device_ids=true, to_apply=%region_5.0 | all-reduce | flops 4096 | bytes 32768 | tf_op jit(solution)/shard_map/psum | solution.py:47
  161.0 31.6 %all-reduce.10.cloned.1.call-done = f32[128,128]{1,0:T(8,128)} async-done(((f32[128,128]{1,0:T(8,128)}), f32[128,128]{1,0:T(8,128)}) %all-reduce.10.cloned.1.call-update) | async-done | bytes 65552 | tf_op jit(solution)/shard_map/psum | solution.py:46
  192.6 1.1 fusion.12
  194.0 1.0 fusion.17
  195.5 23.9 %psum.117 = f32[64,128]{1,0:T(8,128)S(1)} all-reduce(f32[64,128]{1,0:T(8,128)S(1)} %bitcast.76), channel_id=1, replica_groups=mesh['ia'=4,'ja'=4,'ka'=2] {'ja','ka'}, use_global_device_ids=true, to_apply=%region_8.0 | all-reduce | flops 8192 | bytes 65536 | tf_op jit(solution)/shard_map/psum | solution.py:45
  220.0 60.1 %psum.120 = f32[32,128]{1,0:T(8,128)S(1)} all-reduce(f32[32,128]{1,0:T(8,128)S(1)} %bitcast.77), channel_id=1, replica_groups=mesh['ia'=4,'ja'=4,'ka'=2] {'ia','ja'}, use_global_device_ids=true, to_apply=%region_13.0 | all-reduce | flops 4096 | bytes 32768 | tf_op jit(solution)/shard_map/psum | solution.py:47
  282.1 28.3 %all-reduce.14.cloned.1.call-done = f32[128,128]{1,0:T(8,128)} async-done(((f32[128,128]{1,0:T(8,128)}), f32[128,128]{1,0:T(8,128)}) %all-reduce.14.cloned.1.call-update) | async-done | bytes 65552 | tf_op jit(solution)/shard_map/psum | solution.py:46
  310.5 1.5 multiply_reduce_fusion.7
  314.7 40.1 %all-reduce = (f32[]{:T(128)}, f32[]{:T(128)}) all-reduce(f32[]{:T(128)S(6)} %add.131, f32[]{:T(128)S(6)} %add.138), channel_id=1, replica_groups=mesh['ia'=4,'ja'=4,'ka'=2] {'ia','ja','ka'}, use_global_device_ids=true, to_apply=%region_7.0 | all-reduce | flops 2 | bytes 16 | tf_op jit(solution)/shard_map/psum | solution.py:63
  359.9 39.2 %psum.122 = f32[]{:T(128)} all-reduce(f32[]{:T(128)S(6)} %add.140), channel_id=1, replica_groups=mesh['ia'=4,'ja'=4,'ka'=2] {'ia','ja','ka'}, use_global_device_ids=true, to_apply=%region_19.0 | all-reduce | flops 1 | bytes 8 | tf_op jit(solution)/shard_map/psum | solution.py:63
  401.5 1.0 fusion.18
  402.5 60.2 %psum.126 = f32[32,128]{1,0:T(8,128)S(1)} all-reduce(f32[32,128]{1,0:T(8,128)S(1)} %bitcast.79), channel_id=1, replica_groups=mesh['ia'=4,'ja'=4,'ka'=2] {'ia','ja'}, use_global_device_ids=true, to_apply=%region_25.0 | all-reduce | flops 4096 | bytes 32768 | tf_op jit(solution)/shard_map/psum | solution.py:47
  464.1 22.9 %psum.123 = f32[64,128]{1,0:T(8,128)S(1)} all-reduce(f32[64,128]{1,0:T(8,128)S(1)} %bitcast.74), channel_id=1, replica_groups=mesh['ia'=4,'ja'=4,'ka'=2] {'ja','ka'}, use_global_device_ids=true, to_apply=%region_20.0 | all-reduce | flops 8192 | bytes 65536 | tf_op jit(solution)/shard_map/psum | solution.py:45
  487.6 31.4 %all-reduce.18.cloned.1.call-done = f32[128,128]{1,0:T(8,128)} async-done(((f32[128,128]{1,0:T(8,128)}), f32[128,128]{1,0:T(8,128)}) %all-reduce.18.cloned.1.call-update) | async-done | bytes 65552 | tf_op jit(solution)/shard_map/psum | solution.py:46
  519.1 1.5 fusion.6
  521.8 40.1 %psum.127 = f32[]{:T(128)} all-reduce(f32[]{:T(128)S(6)} %add.150), channel_id=1, replica_groups=mesh['ia'=4,'ja'=4,'ka'=2] {'ia','ja','ka'}, use_global_device_ids=true, to_apply=%region_27.0 | all-reduce | flops 1 | bytes 8 | tf_op jit(solution)/shard_map/psum | solution.py:63
  (60 shorter events, 11.0 us)
Async XLA Ops:
  7.2 153.6 %all-reduce.8.cloned.1.call-start = ((), (), s32[]{:S(2)}) async-start(), calls=%async_computation | async-start | bytes 131072 | tf_op jit(solution)/shard_map/psum | solution.py:46
  21.8 0.7 copy-start.3
  44.4 0.7 copy-start.2
  77.0 1.0 copy-start.1
  79.4 113.2 %all-reduce.10.cloned.1.call-start = ((), (), s32[]{:S(2)}) async-start(), calls=%async_computation.1 | async-start | bytes 131072 | tf_op jit(solution)/shard_map/psum | solution.py:46
  160.8 119.4 %all-reduce.12.cloned.1.call-start = ((), (), s32[]{:S(2)}) async-start(), calls=%async_computation.2 | async-start | bytes 131072 | tf_op jit(solution)/shard_map/psum | solution.py:46
  195.3 115.2 %all-reduce.14.cloned.1.call-start = ((), (), s32[]{:S(2)}) async-start(), calls=%async_computation.3 | async-start | bytes 131072 | tf_op jit(solution)/shard_map/psum | solution.py:46
  280.1 30.4 %copy-start = (f32[128,128]{1,0:T(8,128)S(1)}, f32[128,128]{1,0:T(8,128)}, u32[]{:S(2)}) copy-start(f32[128,128]{1,0:T(8,128)} %all-reduce.10.cloned.1.call-done) | copy-start | bytes 196612
  280.1 206.9 %all-reduce.16.cloned.1.call-start = ((), (), s32[]{:S(2)}) async-start(), calls=%async_computation.4 | async-start | bytes 131072 | tf_op jit(solution)/shard_map/psum | solution.py:46
  462.7 56.4 %all-reduce.18.cloned.1.call-start = ((), (), s32[]{:S(2)}) async-start(), calls=%async_computation.5 | async-start | bytes 131072 | tf_op jit(solution)/shard_map/psum | solution.py:46
Sparse Core Ops, SparseCore 0:
  79.5 17.8 all-reduce.7
  160.9 31.6 all-reduce.9
  195.4 20.5 all-reduce.11
  280.3 30.1 all-reduce.13
  462.8 17.2 all-reduce.15
  487.1 31.8 all-reduce.17
